TPU v7x, 512 devices: a whole 4x4x16 slice. The times are simulated.
512 devices in a mesh: win: 8 (over y, core), frame: 64 (over z, x).
Axes of the slice: x: 4, y: 4, z: 16, core: 2. Of those that a mesh axis runs over, the one named last changes fastest.
Arguments:
- distances: float32 [32, 131072], P(None, 'frame'), may hold values from 0.05 to 9
- sample_ids: int32 [131072], P('frame'), may hold values from 0 to 4095, as said below
- lengths: int32 [64], replicated, may hold values from 1 to 2048, 81920 in all
- stiffness: float32 [4096, 32], P('win'), may hold values from 0.5 to 19
- centers: float32 [4096, 32], P('win'), may hold values from 0.1 to 3.7
Outputs:
- free_energy: float32 [4096], P('win')
Inputs may be any that keep to these rules, and one draw needn't show every extreme that they name: The frames of a block occupy its first slots; the lengths add up to 81920 and the largest is 2048. `sample_ids`: slots beyond a block's length hold ids that are not used; exactly 512 windows appear in no slot.
All inputs are finite; a program needn't handle non-finite values.
Results may differ from a plain program's by a relative error of at most 0.0003.
Values sent between devices are 32-bit elements; how exact they have to be, the bound alone decides.
No kernel may reach another device: no remote copies, remote signals or barrier semaphores. Data moves between devices by JAX's collectives and lax.ppermute only.
A program may use at most 64 MiB of HBM per device.

v0:
```python
import jax
import jax.numpy as jnp
from jax import lax
from jax.sharding import PartitionSpec as P

ITERS = 2
BAL = 1280
floor_value = -1e30


def coefficients(stiffness, centers):
    constant = jnp.sum(0.5 * stiffness * centers * centers, axis=1, keepdims=True)
    return jnp.concatenate([constant, -stiffness * centers, 0.5 * stiffness], axis=1)


def features(separations):
    unit_row = jnp.ones((1, separations.shape[1]), separations.dtype)
    return jnp.concatenate([unit_row, separations, separations * separations], axis=0)


def energies(coef_rows, separations):
    return jnp.dot(
        coef_rows,
        features(separations),
        precision=lax.Precision.HIGHEST,
        preferred_element_type=jnp.float32,
    )


def pair_combine(earlier, latter):
    top_all = jnp.maximum(earlier[0], latter[0])
    merged = earlier[1] * jnp.exp(earlier[0] - top_all) + latter[1] * jnp.exp(latter[0] - top_all)
    return (top_all, merged)


def pick_block(slot_total):
    return 512 if slot_total % 512 == 0 else slot_total


def denominators(highest, summed):
    global_top = lax.pmax(highest, "win")
    summed = lax.psum(summed * jnp.exp(highest - global_top), "win")
    highest = global_top
    return highest + jnp.log(summed)


def window_totals(highest, summed):
    global_top = lax.pmax(highest, "frame")
    summed = lax.psum(summed * jnp.exp(highest - global_top), "frame")
    highest = global_top
    return -(highest + jnp.log(summed))


def on_device(distances, sample_ids, lengths, stiffness, centers):
    coef_rows = coefficients(stiffness, centers)
    local_windows = stiffness.shape[0]
    restraints, capacity = distances.shape
    my_index = lax.axis_index("frame")
    own_length = lax.dynamic_index_in_dim(lengths, my_index, keepdims=False)
    slot_index = jnp.arange(capacity, dtype=jnp.int32)
    slot_usable = slot_index < own_length
    numbers = lax.axis_index("win") * local_windows + jnp.arange(local_windows, dtype=jnp.int32)
    count_len = pick_block(capacity)
    id_blocks = sample_ids.reshape(capacity // count_len, count_len)
    use_blocks = slot_usable.reshape(capacity // count_len, count_len)

    def count_block(running, inputs):
        id_block, use_block = inputs
        matches = (id_block[None, :] == numbers[:, None]) & use_block[None, :]
        return (running + jnp.sum(matches.astype(jnp.float32), axis=1), None)

    local_counts, _ = lax.scan(
        count_block, jnp.zeros((local_windows,), jnp.float32), (id_blocks, use_blocks)
    )
    counts = lax.psum(local_counts, "frame")
    frame_devices = lax.axis_size("frame")
    row_count = capacity // frame_devices
    offsets = jnp.cumsum(lengths) - lengths
    own_offset = lax.dynamic_index_in_dim(offsets, my_index, keepdims=False)
    arranged = distances.reshape(restraints, row_count, frame_devices)
    rolled = jnp.roll(arranged, own_offset % frame_devices, axis=2)
    received = lax.all_to_all(rolled, "frame", split_axis=2, concat_axis=2, tiled=True)
    lead_slot = (my_index - offsets) % frame_devices
    delivered = jnp.maximum((lengths - lead_slot + frame_devices - 1) // frame_devices, 0)
    begin_at = jnp.cumsum(delivered) - delivered
    target = jnp.arange(BAL, dtype=jnp.int32)
    source = jnp.sum(((begin_at + delivered)[None, :] <= target[:, None]).astype(jnp.int32), axis=1)
    within = target - jnp.take(begin_at, source)
    received_flat = received.reshape(restraints, row_count * frame_devices)
    frames_here = jnp.take(received_flat, within * frame_devices + source, axis=1)
    usable = jnp.ones((BAL,), jnp.bool_)
    sampled = counts > 0.5
    log_count = jnp.log(jnp.maximum(counts, 1.0))
    slot_total = frames_here.shape[1]
    block_len = pick_block(slot_total)
    block_count = slot_total // block_len
    frame_blocks = frames_here.reshape(restraints, block_count, block_len).transpose(1, 0, 2)
    usable_blocks = usable.reshape(block_count, block_len)
    free_energy = jnp.zeros((local_windows,), jnp.float32)
    for iteration in range(ITERS):
        shifted = log_count + free_energy

        def den_block(separations):
            energy = energies(coef_rows, separations)
            exponent = jnp.where(sampled[:, None], shifted[:, None] - energy, floor_value)
            highest = jnp.max(exponent, axis=0)
            summed = jnp.sum(
                jnp.where(sampled[:, None], jnp.exp(exponent - highest[None, :]), 0.0), axis=0
            )
            return (highest, summed)

        highest, summed = lax.map(den_block, frame_blocks)
        log_den = denominators(highest.reshape(-1), summed.reshape(-1)).reshape(
            block_count, block_len
        )

        def frame_block(running, inputs):
            separations, den_values, use_block = inputs
            energy = energies(coef_rows, separations)
            exponent = jnp.where(use_block[None, :], -energy - den_values[None, :], floor_value)
            block_top = jnp.max(exponent, axis=1)
            block_sum = jnp.sum(
                jnp.where(use_block[None, :], jnp.exp(exponent - block_top[:, None]), 0.0), axis=1
            )
            return (pair_combine(running, (block_top, block_sum)), None)

        start_value = (
            jnp.full((local_windows,), floor_value, jnp.float32),
            jnp.zeros((local_windows,), jnp.float32),
        )
        running, _ = lax.scan(frame_block, start_value, (frame_blocks, log_den, usable_blocks))
        free_energy = window_totals(running[0], running[1])
    return free_energy


def solution(mesh):
    return jax.shard_map(
        on_device,
        mesh=mesh,
        in_specs=(P(None, "frame"), P("frame"), P(), P("win", None), P("win", None)),
        out_specs=P("win"),
        check_vma=False,
    )
```

profile of v0, /device:TPU:2, one launch (start us, length us, event | category | flops | bytes accessed | tf_op | source)
XLA Modules:
  0.0 835.0 jit_solution(18027603402774270897)
XLA Ops:
  0.0 0.7 copy.18
  4.2 1.2 reshape.159
  5.8 0.9 copy.22
  6.7 1.2 reshape.445
  7.9 18.6 %all-to-all-start = ((f32[64,1,1024]{2,1,0:T(1,128)}), f32[64,1,1024]{2,1,0:T(1,128)S(1)}, u32[]{:S(2)}, u32[]{:S(2)}) async-start(f32[64,1,1024]{2,1,0:T(1,128)} %reshape.445), calls=%async_computation | async-start | bytes 524288 | tf_op jit(solution)/shard_map/all_to_all | solution.py:82
  28.3 0.7 fusion.26
  29.0 0.7 fusion.25
  29.7 0.7 fusion.24
  31.1 1.6 while.3
  32.7 139.1 %psum.35 = f32[512]{0:T(512)S(1)} all-reduce(f32[512]{0:T(512)S(1)} %get-tuple-element.89), channel_id=1, replica_groups=mesh['win'=8,'frame'=64] {'frame'}, use_global_device_ids=true, to_apply=%region_7.8 | all-reduce | flops 512 | bytes 4096 | tf_op jit(solution)/shard_map/psum | solution.py:75
  171.8 4.4 fusion.16
  176.2 0.9 compare_reduce_fusion.56
  177.2 35.6 %compare_and_fusion = (pred[1280]{0:T(1024)(128)(4,1)S(1)}, s32[1280]{0:T(1024)S(1)}) fusion(s32[1280]{0:T(1024)S(1)} %convert_reduce_fusion.1, pred[1280]{0:T(1024)(128)(4,1)S(1)} %get-tuple-element.188, pred[1280]{0:T(1024)(128)(4,1)S(1)} %get-tuple-element.186, pred[1280]{0:T(1024)(128)(4,1)S(1)} %get-tuple-element.187, ...), kind=kLoop, calls=%fused_computation.111 | loop fusion | flops 93440 | bytes 89828 | tf_op jit(solution)/shard_map/jit(_take)/and | solution.py:90
  213.5 1.3 reduce.122
  215.7 2.4 gather_fusion
  218.3 2.9 fusion.2
  221.2 12.7 %pmax.28 = f32[1280]{0:T(1024)S(1)} all-reduce(f32[1280]{0:T(1024)S(1)} %get-tuple-element.274), channel_id=1, replica_groups=mesh['win'=8,'frame'=64] {'win'}, use_global_device_ids=true, to_apply=%region_9.10 | all-reduce | flops 1280 | bytes 10240 | tf_op jit(solution)/shard_map/pmax | solution.py:41
  234.6 12.9 %psum.36 = f32[1280]{0:T(1024)S(1)} all-reduce(f32[1280]{0:T(1024)S(1)} %exponential_multiply_fusion.1), channel_id=1, replica_groups=mesh['win'=8,'frame'=64] {'win'}, use_global_device_ids=true, to_apply=%region_11.12 | all-reduce | flops 1280 | bytes 10240 | tf_op jit(solution)/shard_map/psum | solution.py:42
  248.5 142.5 %pmax.29 = f32[512]{0:T(512)S(1)} all-reduce(f32[512]{0:T(512)S(1)} %broadcast_maximum_fusion.1), channel_id=1, replica_groups=mesh['win'=8,'frame'=64] {'frame'}, use_global_device_ids=true, to_apply=%region_13.14 | all-reduce | flops 512 | bytes 4096 | tf_op jit(solution)/shard_map/pmax | solution.py:48
  391.0 138.0 %psum.37 = f32[512]{0:T(512)S(1)} all-reduce(f32[512]{0:T(512)S(1)} %exponential_multiply_fusion.3), channel_id=1, replica_groups=mesh['win'=8,'frame'=64] {'frame'}, use_global_device_ids=true, to_apply=%region_15.16 | all-reduce | flops 512 | bytes 4096 | tf_op jit(solution)/shard_map/psum | solution.py:49
  530.0 12.7 %pmax.30 = f32[1280]{0:T(1024)S(1)} all-reduce(f32[1280]{0:T(1024)S(1)} %fusion.3), channel_id=1, replica_groups=mesh['win'=8,'frame'=64] {'win'}, use_global_device_ids=true, to_apply=%region_17.18 | all-reduce | flops 1280 | bytes 10240 | tf_op jit(solution)/shard_map/pmax | solution.py:41
  542.7 12.7 %psum.38 = f32[1280]{0:T(1024)S(1)} all-reduce(f32[1280]{0:T(1024)S(1)} %exponential_multiply_fusion), channel_id=1, replica_groups=mesh['win'=8,'frame'=64] {'win'}, use_global_device_ids=true, to_apply=%region_19.20 | all-reduce | flops 1280 | bytes 10240 | tf_op jit(solution)/shard_map/psum | solution.py:42
  556.4 140.0 %pmax.31 = f32[512]{0:T(512)S(1)} all-reduce(f32[512]{0:T(512)S(1)} %broadcast_maximum_fusion), channel_id=1, replica_groups=mesh['win'=8,'frame'=64] {'frame'}, use_global_device_ids=true, to_apply=%region_21.22 | all-reduce | flops 512 | bytes 4096 | tf_op jit(solution)/shard_map/pmax | solution.py:48
  696.4 138.0 %psum.39 = f32[512]{0:T(512)S(1)} all-reduce(f32[512]{0:T(512)S(1)} %exponential_multiply_fusion.2), channel_id=1, replica_groups=mesh['win'=8,'frame'=64] {'frame'}, use_global_device_ids=true, to_apply=%region_23.24 | all-reduce | flops 512 | bytes 4096 | tf_op jit(solution)/shard_map/psum | solution.py:49
  (71 shorter events, 11.8 us)
Async XLA Ops:
  4.2 22.3 %copy-start.3 = (s32[64]{0:T(128)S(1)}, s32[64]{0:T(128)}, u32[]{:S(2)}) copy-start(s32[64]{0:T(128)} %param.9) | copy-start | bytes 772
  4.2 26.9 %copy-start.2 = (s32[2048]{0:T(1024)S(1)}, s32[2048]{0:T(1024)}, u32[]{:S(2)}) copy-start(s32[2048]{0:T(1024)} %param.8) | copy-start | bytes 24580
  5.4 207.5 %copy-start = (f32[512,32]{0,1:T(8,128)S(1)}, f32[512,32]{0,1:T(8,128)}, u32[]{:S(2)}) copy-start(f32[512,32]{0,1:T(8,128)} %param.11) | copy-start | bytes 196612
  5.4 207.5 %copy-start.1 = (f32[512,32]{0,1:T(8,128)S(1)}, f32[512,32]{0,1:T(8,128)}, u32[]{:S(2)}) copy-start(f32[512,32]{0,1:T(8,128)} %param.10) | copy-start | bytes 196612
  7.9 205.1 %all-to-all-start = ((f32[64,1,1024]{2,1,0:T(1,128)}), f32[64,1,1024]{2,1,0:T(1,128)S(1)}, u32[]{:S(2)}, u32[]{:S(2)}) async-start(f32[64,1,1024]{2,1,0:T(1,128)} %reshape.445), calls=%async_computation | async-start | bytes 524288 | tf_op jit(solution)/shard_map/all_to_all | solution.py:82
where the time goes:
time: 836 us; the launch traced here: 835 us
  blocking collectives  748 us (89%)
  other arithmetic  50.4 us (6%)
  starting transfers between devices  18.6 us (2%)
  local copies, waits for them, and re-layouts  12.1 us (1%)
    pmax x2, blocking collectives, window_totals(): global_top = lax.pmax(highest, 'frame')  282 us
    psum x2, blocking collectives, window_totals(): summed = lax.psum(summed * jnp.exp(highest - global_top), 'frame')  276 us
    psum x1, blocking collectives, on_device(): counts = lax.psum(local_counts, 'frame')  139 us
    and x1, other arithmetic, on_device(): jnp.take(received_flat, within * frame_devices + source, axis=1)  35.6 us
    psum x2, blocking collectives, denominators(): summed = lax.psum(summed * jnp.exp(highest - global_top), 'win')  25.6 us
    pmax x2, blocking collectives, denominators(): global_top = lax.pmax(highest, 'win')  25.3 us
    all_to_all x1, starting transfers between devices, on_device(): lax.all_to_all(rolled, 'frame', split_axis=2, concat_axis=2, tiled=True)  18.6 us
  transfers between devices with their start and end apart: 1, of which 0 were waited for; matrix products, arithmetic and copies ran while one was open for 6% of the time, Pallas kernels for 0%

commit v1 on v0

--- a/solution.py
+++ b/solution.py
@@ -6,6 +6,12 @@
 ITERS = 2
 BAL = 1280
 floor_value = -1e30
+
+
+def view_object(base_x):
+    arr_now = lax.all_gather(base_x, "frame")
+    b_now = jnp.sum(arr_now, axis=0)
+    return b_now
 
 
 def coefficients(stiffness, centers):
@@ -46,7 +52,7 @@
 
 def window_totals(highest, summed):
     global_top = lax.pmax(highest, "frame")
-    summed = lax.psum(summed * jnp.exp(highest - global_top), "frame")
+    summed = view_object(summed * jnp.exp(highest - global_top))
     highest = global_top
     return -(highest + jnp.log(summed))
 

time: 836 us -> 755 us (0.903)
  blocking collectives: 748 us -> 668 us
    psum x2 -> x0, blocking collectives: 276 us -> none  [window_totals(): summed = lax.psum(summed * jnp.exp(highest - global_top), 'frame')]
    all_gather x0 -> x2, blocking collectives: none -> 195 us  [view_object(): arr_now = lax.all_gather(base_x, 'frame')]
where the time goes in v1:
time: 755 us; the launch traced here: 754 us
  blocking collectives  668 us (88%)
  other arithmetic  50.7 us (7%)
  starting transfers between devices  18.6 us (2%)
  local copies, waits for them, and re-layouts  12.1 us (2%)
    pmax x2, blocking collectives, window_totals(): global_top = lax.pmax(highest, 'frame')  282 us
    all_gather x2, blocking collectives, view_object(): arr_now = lax.all_gather(base_x, 'frame')  195 us
    psum x1, blocking collectives, on_device(): counts = lax.psum(local_counts, 'frame')  139 us
    and x1, other arithmetic, on_device(): jnp.take(received_flat, within * frame_devices + source, axis=1)  35.6 us
    psum x2, blocking collectives, denominators(): summed = lax.psum(summed * jnp.exp(highest - global_top), 'win')  25.6 us
    pmax x2, blocking collectives, denominators(): global_top = lax.pmax(highest, 'win')  25.3 us
    all_to_all x1, starting transfers between devices, on_device(): lax.all_to_all(rolled, 'frame', split_axis=2, concat_axis=2, tiled=True)  18.6 us
  transfers between devices with their start and end apart: 1, of which 0 were waited for; matrix products, arithmetic and copies ran while one was open for 6% of the time, Pallas kernels for 0%

profile of v1, /device:TPU:2, one launch (start us, length us, event | category | flops | bytes accessed | tf_op | source)
XLA Modules:
  0.0 754.3 jit_solution(914710049426218248)
XLA Ops:
  0.0 0.7 copy.18
  4.2 1.2 reshape.159
  5.8 0.9 copy.22
  6.7 1.2 reshape.453
  7.9 18.6 %all-to-all-start = ((f32[64,1,1024]{2,1,0:T(1,128)}), f32[64,1,1024]{2,1,0:T(1,128)S(1)}, u32[]{:S(2)}, u32[]{:S(2)}) async-start(f32[64,1,1024]{2,1,0:T(1,128)} %reshape.453), calls=%async_computation | async-start | bytes 524288 | tf_op jit(solution)/shard_map/all_to_all | solution.py:88
  28.3 0.7 fusion.26
  29.0 0.7 fusion.25
  29.7 0.7 fusion.24
  31.1 1.6 while.3
  32.7 139.1 %psum.21 = f32[512]{0:T(512)S(1)} all-reduce(f32[512]{0:T(512)S(1)} %get-tuple-element.89), channel_id=1, replica_groups=mesh['win'=8,'frame'=64] {'frame'}, use_global_device_ids=true, to_apply=%region_7.8 | all-reduce | flops 512 | bytes 4096 | tf_op jit(solution)/shard_map/psum | solution.py:81
  171.8 4.4 fusion.16
  176.2 0.9 compare_reduce_fusion.56
  177.2 35.6 %compare_and_fusion = (pred[1280]{0:T(1024)(128)(4,1)S(1)}, s32[1280]{0:T(1024)S(1)}) fusion(s32[1280]{0:T(1024)S(1)} %convert_reduce_fusion.1, pred[1280]{0:T(1024)(128)(4,1)S(1)} %get-tuple-element.188, pred[1280]{0:T(1024)(128)(4,1)S(1)} %get-tuple-element.186, pred[1280]{0:T(1024)(128)(4,1)S(1)} %get-tuple-element.187, ...), kind=kLoop, calls=%fused_computation.111 | loop fusion | flops 93440 | bytes 89828 | tf_op jit(solution)/shard_map/jit(_take)/and | solution.py:96
  213.5 1.3 reduce.124
  215.7 2.4 gather_fusion
  218.3 2.9 fusion.2
  221.2 12.7 %pmax.28 = f32[1280]{0:T(1024)S(1)} all-reduce(f32[1280]{0:T(1024)S(1)} %get-tuple-element.274), channel_id=1, replica_groups=mesh['win'=8,'frame'=64] {'win'}, use_global_device_ids=true, to_apply=%region_9.10 | all-reduce | flops 1280 | bytes 10240 | tf_op jit(solution)/shard_map/pmax | solution.py:47
  234.6 12.9 %psum.22 = f32[1280]{0:T(1024)S(1)} all-reduce(f32[1280]{0:T(1024)S(1)} %exponential_multiply_fusion.1), channel_id=1, replica_groups=mesh['win'=8,'frame'=64] {'win'}, use_global_device_ids=true, to_apply=%region_11.12 | all-reduce | flops 1280 | bytes 10240 | tf_op jit(solution)/shard_map/psum | solution.py:48
  248.5 142.5 %pmax.29 = f32[512]{0:T(512)S(1)} all-reduce(f32[512]{0:T(512)S(1)} %broadcast_maximum_fusion.1), channel_id=1, replica_groups=mesh['win'=8,'frame'=64] {'frame'}, use_global_device_ids=true, to_apply=%region_13.14 | all-reduce | flops 512 | bytes 4096 | tf_op jit(solution)/shard_map/pmax | solution.py:54
  391.0 96.5 %all-gather.2 = f32[64,1,512]{2,1,0:T(1,128)S(1)} all-gather(f32[1,1,512]{2,1,0:T(1,128)S(1)} %bitcast.86), channel_id=2, replica_groups=mesh['win'=8,'frame'=64] {'frame'}, dimensions={0}, use_global_device_ids=true | all-gather | bytes 133120 | tf_op jit(solution)/shard_map/all_gather | solution.py:12
  488.6 12.7 %pmax.30 = f32[1280]{0:T(1024)S(1)} all-reduce(f32[1280]{0:T(1024)S(1)} %fusion.3), channel_id=1, replica_groups=mesh['win'=8,'frame'=64] {'win'}, use_global_device_ids=true, to_apply=%region_17.18 | all-reduce | flops 1280 | bytes 10240 | tf_op jit(solution)/shard_map/pmax | solution.py:47
  501.3 12.7 %psum.23 = f32[1280]{0:T(1024)S(1)} all-reduce(f32[1280]{0:T(1024)S(1)} %exponential_multiply_fusion), channel_id=1, replica_groups=mesh['win'=8,'frame'=64] {'win'}, use_global_device_ids=true, to_apply=%region_19.20 | all-reduce | flops 1280 | bytes 10240 | tf_op jit(solution)/shard_map/psum | solution.py:48
  515.0 140.0 %pmax.31 = f32[512]{0:T(512)S(1)} all-reduce(f32[512]{0:T(512)S(1)} %broadcast_maximum_fusion), channel_id=1, replica_groups=mesh['win'=8,'frame'=64] {'frame'}, use_global_device_ids=true, to_apply=%region_21.22 | all-reduce | flops 512 | bytes 4096 | tf_op jit(solution)/shard_map/pmax | solution.py:54
  655.0 98.6 %all-gather.3 = f32[64,1,512]{2,1,0:T(1,128)S(1)} all-gather(f32[1,1,512]{2,1,0:T(1,128)S(1)} %bitcast.87), channel_id=3, replica_groups=mesh['win'=8,'frame'=64] {'frame'}, dimensions={0}, use_global_device_ids=true | all-gather | bytes 133120 | tf_op jit(solution)/shard_map/all_gather | solution.py:12
  (73 shorter events, 12.1 us)
Async XLA Ops:
  4.2 22.3 %copy-start.3 = (s32[64]{0:T(128)S(1)}, s32[64]{0:T(128)}, u32[]{:S(2)}) copy-start(s32[64]{0:T(128)} %param.9) | copy-start | bytes 772
  4.2 26.9 %copy-start.2 = (s32[2048]{0:T(1024)S(1)}, s32[2048]{0:T(1024)}, u32[]{:S(2)}) copy-start(s32[2048]{0:T(1024)} %param.8) | copy-start | bytes 24580
  5.4 207.5 %copy-start = (f32[512,32]{0,1:T(8,128)S(1)}, f32[512,32]{0,1:T(8,128)}, u32[]{:S(2)}) copy-start(f32[512,32]{0,1:T(8,128)} %param.11) | copy-start | bytes 196612
  5.4 207.5 %copy-start.1 = (f32[512,32]{0,1:T(8,128)S(1)}, f32[512,32]{0,1:T(8,128)}, u32[]{:S(2)}) copy-start(f32[512,32]{0,1:T(8,128)} %param.10) | copy-start | bytes 196612
  7.9 205.1 %all-to-all-start = ((f32[64,1,1024]{2,1,0:T(1,128)}), f32[64,1,1024]{2,1,0:T(1,128)S(1)}, u32[]{:S(2)}, u32[]{:S(2)}) async-start(f32[64,1,1024]{2,1,0:T(1,128)} %reshape.453), calls=%async_computation | async-start | bytes 524288 | tf_op jit(solution)/shard_map/all_to_all | solution.py:88
